TPU v7x, 32 devices: a whole 2x2x4 slice. The times are simulated.
32 devices in a mesh: chan: 8 (over z, x), band: 4 (over y, core).
Axes of the slice: x: 2, y: 2, z: 4, core: 2. Of those that a mesh axis runs over, the one named last changes fastest.
Arguments:
- spectra: bfloat16 [8, 2, 4096, 512], P('band', None, 'chan'), may hold values from -64 to 64
- half_width: int32 [512], replicated, may hold values from 1 to 32, as said below
- panel_block: int32 [4], replicated, may hold values from 0 to 7
- panel_offset: int32 [4], replicated, may hold values from 0 to 256
Outputs:
- cross: bfloat16 [4, 8, 2, 4096, 256], P(None, 'band', None, 'chan')
Inputs may be any that keep to these rules, and one draw needn't show every extreme that they name: `half_width`: some window's half-width is exactly 32.
All inputs are finite; a program needn't handle non-finite values.
Results may differ from a plain program's by a relative error of at most 0.0056.
Values may be sent and summed in bfloat16 or wider, within the bound.
No kernel may reach another device: no remote copies, remote signals or barrier semaphores. Data moves between devices by JAX's collectives and lax.ppermute only.
A program may use at most 64 MiB of HBM per device.

v0:
```python
import jax
import jax.numpy as jnp
from jax import lax
from jax.sharding import PartitionSpec as P

PANEL = 256
NPANEL = 4
HALO = 32


def with_halo(block, sides, width):
    for axis, dim in sides:
        count = lax.axis_size(axis)
        forward = [(i, i + 1) for i in range(count - 1)]
        backward = [(target, source) for source, target in forward]
        low = lax.ppermute(
            lax.slice_in_dim(block, block.shape[dim] - width, None, axis=dim), axis, forward
        )
        high = lax.ppermute(lax.slice_in_dim(block, 0, width, axis=dim), axis, backward)
        block = jnp.concatenate([low, block, high], axis=dim)
    return block


def from_root(block, axis, holder):
    block = jnp.where(lax.axis_index(axis) == holder, block, jnp.zeros_like(block))
    return lax.psum(block, axis)


def norm_scale(power, widths, first_chan, channels, bins):
    rows = power.shape[0]
    padded = with_halo(power, (("chan", 0),), HALO)
    total = jnp.zeros_like(power)
    for offset in range(-HALO, HALO + 1):
        window = padded[HALO + offset : HALO + offset + rows]
        total = total + jnp.where(abs(offset) <= widths[None, :], window, jnp.float32(0.0))
    chan_index = jnp.arange(rows, dtype=jnp.int32)[:, None] + first_chan
    count = (
        jnp.minimum(chan_index + widths[None, :], channels - 1)
        - jnp.maximum(chan_index - widths[None, :], 0)
        + 1
    )
    return lax.rsqrt(total / (count.astype(jnp.float32) * bins) + 1e-06)


def local(spectra, half_width, panel_block, panel_offset):
    f_dev, parts, ch_dev, windows = spectra.shape
    bins = f_dev * lax.axis_size("band")
    channels = ch_dev * lax.axis_size("chan")
    block_here = lax.axis_index("chan")
    first_chan = block_here * ch_dev
    local_power = jnp.sum(jnp.square(spectra.astype(jnp.float32)), axis=(0, 1))
    share = lax.psum_scatter(local_power, "band", scatter_dimension=1, tiled=True)
    share_width = share.shape[1]
    widths = lax.dynamic_slice_in_dim(half_width, lax.axis_index("band") * share_width, share_width)
    scale_share = norm_scale(share, widths, first_chan, channels, bins)
    scale = lax.all_gather(scale_share, "band", axis=1, tiled=True)
    normed = (spectra.astype(jnp.float32) * scale[None, None]).astype(jnp.bfloat16)
    flat = normed.reshape(f_dev, 2 * ch_dev, windows)
    results = []
    for panel in range(NPANEL):
        source = from_root(
            lax.dynamic_slice_in_dim(normed, panel_offset[panel], PANEL, 2),
            "chan",
            panel_block[panel],
        )
        right = source.reshape(f_dev, 2 * PANEL, windows)
        grams = jnp.einsum("fxw,fyw->fxy", flat, right, preferred_element_type=jnp.float32)
        real_part = grams[:, :ch_dev, :PANEL] + grams[:, ch_dev:, PANEL:]
        imag_part = grams[:, ch_dev:, :PANEL] - grams[:, :ch_dev, PANEL:]
        results.append(
            (jnp.stack([real_part, imag_part], axis=1) * windows ** (-0.5)).astype(jnp.bfloat16)
        )
    return jnp.stack(results)


def solution(mesh):
    placed = (P("band", None, "chan", None), P(), P(), P())
    return jax.shard_map(
        local,
        mesh=mesh,
        in_specs=placed,
        out_specs=P(None, "band", None, "chan", None),
        check_vma=False,
    )
```

profile of v0, /device:TPU:0, one launch (start us, length us, event | category | flops | bytes accessed | tf_op | source)
XLA Modules:
  0.0 251.9 jit_solution(6635391899001738447)
XLA Ops:
  6.5 3.1 %fusion = f32[512,512]{1,0:T(8,128)} fusion(bf16[2,2,512,512]{3,2,1,0:T(8,128)(2,1)} %param.4), kind=kLoop, calls=%fused_computation.2 | loop fusion | flops 2883584 | bytes 3145728 | tf_op jit(solution)/shard_map/reduce_sum | solution.py:51
  9.7 0.8 broadcast_compare_fusion.32
  10.5 26.9 %reduce-scatter.2.cloned.1.call-done = f32[512,128]{1,0:T(8,128)} async-done(((f32[512,512]{1,0:T(8,128)}), f32[512,128]{1,0:T(8,128)}) %reduce-scatter.2.cloned.1.call-update) | async-done | bytes 262160 | tf_op jit(solution)/shard_map/reduce_scatter | solution.py:52
  37.4 0.7 fusion.81
  38.1 3.3 %collective-permute-start = (f32[32,128]{1,0:T(8,128)S(1)}, f32[32,128]{1,0:T(8,128)S(1)}, u32[]{:S(2)}, u32[]{:S(2)}) collective-permute-start(f32[32,128]{1,0:T(8,128)S(1)} %get-tuple-element.25), channel_id=1, source_target_pairs={{0,4},{4,8},{8,12},{12,16},{16,20},{20,24},{24,28},{1,5},{5,9},{9,... | collective-permute-start | bytes 49160 | tf_op jit(solution)/shard_map/ppermute | solution.py:16
  41.5 1.3 collective-permute-start.1
  42.9 1.0 constant_dynamic-update-slice_fusion
  43.9 3.2 %collective-permute-done.1 = f32[32,128]{1,0:T(8,128)S(1)} collective-permute-done((f32[32,128]{1,0:T(8,128)S(1)}, f32[32,128]{1,0:T(8,128)S(1)}, u32[]{:S(2)}, u32[]{:S(2)}) %collective-permute-start.1) | collective-permute-done | bytes 16416 | tf_op jit(solution)/shard_map/ppermute | solution.py:19
  47.1 4.8 %fusion.17 = f32[512,128]{1,0:T(8,128)} fusion(f32[544,128]{1,0:T(8,128)S(1)} %constant_dynamic-update-slice_fusion.2, f32[544,128]{1,0:T(8,128)S(1)} %get-tuple-element.23, f32[512,128]{1,0:T(8,128)} %reduce-scatter.2.cloned.1.call-done, s32[128]{0:T(128)S(1)} %get-tuple-element.10, s32[512]{0:T(512)S(1)} %iota_add_fusion, ...), kind=kLoop, calls=%fused_computation.37 | loop fusion | flops 9109504 | bytes 17308288 | tf_op jit(solution)/shard_map/rsqrt | solution.py:42
  52.0 0.7 fusion.83
  57.8 0.6 fusion.82
  63.5 5.5 %all-gather.2.cloned.1.call-done = f32[512,512]{1,0:T(8,128)} async-done(((f32[512,128]{1,0:T(8,128)}), f32[512,512]{1,0:T(8,128)}) %all-gather.2.cloned.1.call-update) | async-done | bytes 1048592 | tf_op jit(solution)/shard_map/all_gather | solution.py:56
  68.9 2.3 fusion.1
  71.2 3.1 %dynamic-slice_select_fusion.3 = (bf16[2,2,256,512]{3,2,1,0:T(8,128)(2,1)}, bf16[2,2,256,512]{3,2,1,0:T(8,128)(2,1)}, bf16[2,2,256,512]{3,2,1,0:T(8,128)(2,1)}, bf16[2,2,256,512]{3,2,1,0:T(8,128)(2,1)}) fusion(bf16[2,2,512,512]{3,2,1,0:T(8,128)(2,1)S(1)} %fusion.1, s32[]{:T(128)S(6)} %select_n.304, pred[]{:T(512)S(6)} %eq.12, s32[]{:T(128)S(6)} %select_n.313, ...), kind=kLoop, calls=%fused_computation.32 | loop fusion | flops 2097152 | bytes 8388628 | tf_op jit(solution)/shard_map/jit(_where)/select_n | solution.py:25
  74.4 156.6 %all-reduce.3.cloned.1.call-done = (bf16[2,512,512]{2,1,0:T(8,128)(2,1)}, bf16[2,512,512]{2,1,0:T(8,128)(2,1)}, bf16[2,512,512]{2,1,0:T(8,128)(2,1)}, bf16[2,512,512]{2,1,0:T(8,128)(2,1)}) async-done(((bf16[2,512,512]{2,1,0:T(8,128)(2,1)}, bf16[2,512,512]{2,1,0:T(8,128)(2,1)}, bf16[2,512,512]{2,1,0:T(8,128)(2,1)}, bf16[2,512,512]{2,1,0:T(8,128)(2,1)}), (bf16[2,512,512]{2,1,0:T(8,128)(2,1)}, ...) | async-done | bytes 4194320 | tf_op jit(solution)/shard_map/psum | solution.py:26
  231.0 2.5 fusion.87
  233.8 0.9 copy-done.2
  234.7 1.3 fusion.86
  236.3 0.9 copy-done.1
  237.3 1.3 fusion.85
  238.8 0.9 copy-done
  239.8 1.3 fusion.84
  242.4 0.6 pad_maximum_fusion
  243.0 2.3 copy.5
  (24 shorter events, 2.4 us)
Async XLA Ops:
  6.5 30.9 %reduce-scatter.2.cloned.1.call-start = ((), (), s32[]{:S(2)}) async-start(), calls=%async_computation.1 | async-start | bytes 1310720 | tf_op jit(solution)/shard_map/reduce_scatter | solution.py:52
  9.7 59.3 %all-gather.2.cloned.1.call-start = ((), (), s32[]{:S(2)}) async-start(), calls=%async_computation.2 | async-start | bytes 1310720 | tf_op jit(solution)/shard_map/all_gather | solution.py:56
  38.1 4.8 %collective-permute-start = (f32[32,128]{1,0:T(8,128)S(1)}, f32[32,128]{1,0:T(8,128)S(1)}, u32[]{:S(2)}, u32[]{:S(2)}) collective-permute-start(f32[32,128]{1,0:T(8,128)S(1)} %get-tuple-element.25), channel_id=1, source_target_pairs={{0,4},{4,8},{8,12},{12,16},{16,20},{20,24},{24,28},{1,5},{5,9},{9,... | collective-permute-start | bytes 49160 | tf_op jit(solution)/shard_map/ppermute | solution.py:16
  41.5 5.6 %collective-permute-start.1 = (f32[32,128]{1,0:T(8,128)S(1)}, f32[32,128]{1,0:T(8,128)S(1)}, u32[]{:S(2)}, u32[]{:S(2)}) collective-permute-start(f32[32,128]{1,0:T(8,128)S(1)} %get-tuple-element.26), channel_id=1, source_target_pairs={{4,0},{8,4},{12,8},{16,12},{20,16},{24,20},{28,24},{5,1},{9,5},{13... | collective-permute-start | bytes 49160 | tf_op jit(solution)/shard_map/ppermute | solution.py:19
  47.1 4.9 %copy-start.3 = (s32[4]{0:T(128)S(1)}, s32[4]{0:T(128)}, u32[]{:S(2)}) copy-start(s32[4]{0:T(128)} %param.7) | copy-start | bytes 52
  47.1 10.7 %copy-start.4 = (s32[4]{0:T(128)S(1)}, s32[4]{0:T(128)}, u32[]{:S(2)}) copy-start(s32[4]{0:T(128)} %param.6) | copy-start | bytes 52
  52.0 179.1 %all-reduce.3.cloned.1.call-start = ((), (), s32[]{:S(2)}) async-start(), calls=%async_computation.3 | async-start | bytes 8388608 | tf_op jit(solution)/shard_map/psum | solution.py:26
  233.5 1.2 copy-start.2
  236.0 1.2 copy-start.1
  238.5 1.2 copy-start
Sparse Core Ops, SparseCore 0:
  9.9 27.4 reduce-scatter.1
  52.1 16.8 all-gather.1
  74.5 156.4 all-reduce.2
where the time goes:
time: 252 us
  waiting for transfers between devices  192 us (76%)
  between operations  23.4 us (9%)
  other arithmetic  16.8 us (7%)
  local copies, waits for them, and re-layouts  8.2 us (3%)
  matrix products  6.34 us (3%)
  starting transfers between devices  4.72 us (2%)
    psum x1, waiting for transfers between devices, from_root(): return lax.psum(block, axis)  157 us
    reduce_scatter x1, waiting for transfers between devices, local(): lax.psum_scatter(local_power, 'band', scatter_dimension=1, tiled=True)  26.9 us
    dot_general x4, matrix products, local(): jnp.einsum('fxw,fyw->fxy', flat, right, preferred_element_type=jnp.float32)  6.34 us
    all_gather x1, waiting for transfers between devices, local(): scale = lax.all_gather(scale_share, 'band', axis=1, tiled=True)  5.46 us
  transfers between devices with their start and end apart: 5, of which 5 were waited for; matrix products, arithmetic and copies ran while one was open for 1% of the time, Pallas kernels for 0%

commit v1 on v0

--- a/solution.py
+++ b/solution.py
@@ -23,7 +23,7 @@
 
 def from_root(block, axis, holder):
     block = jnp.where(lax.axis_index(axis) == holder, block, jnp.zeros_like(block))
-    return lax.psum(block, axis)
+    return jnp.sum(lax.all_gather(block, axis), axis=0)
 
 
 def norm_scale(power, widths, first_chan, channels, bins):

time: 252 us -> 600 us (2.38)
  waiting for transfers between devices: 192 us -> 517 us
  other arithmetic: 16.8 us -> 39.7 us
    all_gather x0 -> x4, waiting for transfers between devices: none -> 480 us  [from_root(): return jnp.sum(lax.all_gather(block, axis), axis=0)]
    psum x1 -> x0, waiting for transfers between devices: 157 us -> none  [from_root(): return lax.psum(block, axis)]
    reduce_sum x0 -> x4, other arithmetic: none -> 22.8 us  [from_root(): return jnp.sum(lax.all_gather(block, axis), axis=0)]
  transfers between devices with their start and end apart: 5 -> 8, of which waited for: 5 -> 8; matrix products, arithmetic and copies ran while one was open for 1% -> 3% of each run, Pallas kernels for 0% -> 0%
where the time goes in v1:
time: 600 us; the launch traced here: 599 us
  waiting for transfers between devices  517 us (86%)
  other arithmetic  39.7 us (7%)
  between operations  23.6 us (4%)
  local copies, waits for them, and re-layouts  7.24 us (1%)
  matrix products  6.34 us (1%)
    all_gather x4, waiting for transfers between devices, from_root(): return jnp.sum(lax.all_gather(block, axis), axis=0)  480 us
    reduce_scatter x1, waiting for transfers between devices, local(): lax.psum_scatter(local_power, 'band', scatter_dimension=1, tiled=True)  26.9 us
    reduce_sum x4, other arithmetic, from_root(): return jnp.sum(lax.all_gather(block, axis), axis=0)  22.8 us
  transfers between devices with their start and end apart: 8, of which 8 were waited for; matrix products, arithmetic and copies ran while one was open for 3% of the time, Pallas kernels for 0%

profile of v1, /device:TPU:0, one launch (start us, length us, event | category | flops | bytes accessed | tf_op | source)
XLA Modules:
  0.0 599.3 jit_solution(13967705262658236777)
XLA Ops:
  6.5 3.1 fusion
  10.5 26.9 %reduce-scatter.2.cloned.1.call-done = f32[512,128]{1,0:T(8,128)} async-done(((f32[512,512]{1,0:T(8,128)}), f32[512,128]{1,0:T(8,128)}) %reduce-scatter.2.cloned.1.call-update) | async-done | bytes 262160 | tf_op jit(solution)/shard_map/reduce_scatter | solution.py:52
  38.1 3.3 collective-permute-start
  41.5 1.3 collective-permute-start.1
  42.9 1.0 constant_dynamic-update-slice_fusion
  43.9 3.2 collective-permute-done.1
  47.1 4.8 fusion.17
  63.3 5.6 all-gather.10.cloned.1.call-done
  68.9 2.3 fusion.1
  71.2 3.1 dynamic-slice_select_fusion.3
  76.1 122.9 %all-gather.12.cloned.1.call-done = bf16[16,2,256,512]{3,2,1,0:T(8,128)(2,1)} async-done(((bf16[2,2,256,512]{3,2,1,0:T(8,128)(2,1)}), bf16[16,2,256,512]{3,2,1,0:T(8,128)(2,1)}) %all-gather.12.cloned.1.call-update) | async-done | bytes 8388624 | tf_op jit(solution)/shard_map/all_gather | solution.py:26
  199.0 4.8 reduce_sum.58
  203.8 119.9 %all-gather.18.cloned.1.call-done = bf16[16,2,256,512]{3,2,1,0:T(8,128)(2,1)} async-done(((bf16[2,2,256,512]{3,2,1,0:T(8,128)(2,1)}), bf16[16,2,256,512]{3,2,1,0:T(8,128)(2,1)}) %all-gather.18.cloned.1.call-update) | async-done | bytes 8388624 | tf_op jit(solution)/shard_map/all_gather | solution.py:26
  323.7 6.0 %reduce_sum.61 = bf16[2,2,256,512]{3,2,1,0:T(8,128)(2,1)} reduce(bf16[8,2,2,256,512]{4,3,2,1,0:T(8,128)(2,1)} %bitcast.46, bf16[]{:T(256)} %constant.96.clone.1), dimensions={0}, to_apply=%region_5.6 | reduce | flops 3670016 | bytes 9437186 | tf_op jit(solution)/shard_map/reduce_sum | solution.py:26
  329.7 118.6 %all-gather.16.cloned.1.call-done = bf16[16,2,256,512]{3,2,1,0:T(8,128)(2,1)} async-done(((bf16[2,2,256,512]{3,2,1,0:T(8,128)(2,1)}), bf16[16,2,256,512]{3,2,1,0:T(8,128)(2,1)}) %all-gather.16.cloned.1.call-update) | async-done | bytes 8388624 | tf_op jit(solution)/shard_map/all_gather | solution.py:26
  448.3 6.0 reduce_sum.60
  454.3 118.7 %all-gather.14.cloned.1.call-done = bf16[16,2,256,512]{3,2,1,0:T(8,128)(2,1)} async-done(((bf16[2,2,256,512]{3,2,1,0:T(8,128)(2,1)}), bf16[16,2,256,512]{3,2,1,0:T(8,128)(2,1)}) %all-gather.14.cloned.1.call-update) | async-done | bytes 8388624 | tf_op jit(solution)/shard_map/all_gather | solution.py:26
  573.0 6.0 %reduce_sum.59 = bf16[2,2,256,512]{3,2,1,0:T(8,128)(2,1)} reduce(bf16[8,2,2,256,512]{4,3,2,1,0:T(8,128)(2,1)} %bitcast.48, bf16[]{:T(256)} %constant.96.clone.1), dimensions={0}, to_apply=%region_3.4 | reduce | flops 3670016 | bytes 9437186 | tf_op jit(solution)/shard_map/reduce_sum | solution.py:26
  579.1 2.5 fusion.85
  581.8 0.9 copy-done.1
  582.8 1.3 fusion.86
  585.3 1.3 fusion.87
  586.9 1.3 fusion.84
  590.1 2.3 copy.6
  (35 shorter events, 8.5 us)
Async XLA Ops:
  6.5 30.9 %reduce-scatter.2.cloned.1.call-start = ((), (), s32[]{:S(2)}) async-start(), calls=%async_computation.1 | async-start | bytes 1310720 | tf_op jit(solution)/shard_map/reduce_scatter | solution.py:52
  9.7 59.3 %all-gather.10.cloned.1.call-start = ((), (), s32[]{:S(2)}) async-start(), calls=%async_computation.2 | async-start | bytes 1310720 | tf_op jit(solution)/shard_map/all_gather | solution.py:56
  38.1 4.8 collective-permute-start
  41.5 5.6 collective-permute-start.1
  47.1 4.9 copy-start.2
  47.1 10.5 %copy-start.3 = (s32[4]{0:T(128)S(1)}, s32[4]{0:T(128)}, u32[]{:S(2)}) copy-start(s32[4]{0:T(128)} %param.6) | copy-start | bytes 52
  52.0 147.0 %all-gather.12.cloned.1.call-start = ((), (), s32[]{:S(2)}) async-start(), calls=%async_computation.3 | async-start | bytes 9437184 | tf_op jit(solution)/shard_map/all_gather | solution.py:26
  74.4 249.3 %all-gather.18.cloned.1.call-start = ((), (), s32[]{:S(2)}) async-start(), calls=%async_computation.6 | async-start | bytes 9437184 | tf_op jit(solution)/shard_map/all_gather | solution.py:26
  75.0 373.4 %all-gather.16.cloned.1.call-start = ((), (), s32[]{:S(2)}) async-start(), calls=%async_computation.5 | async-start | bytes 9437184 | tf_op jit(solution)/shard_map/all_gather | solution.py:26
  75.6 497.5 %all-gather.14.cloned.1.call-start = ((), (), s32[]{:S(2)}) async-start(), calls=%async_computation.4 | async-start | bytes 9437184 | tf_op jit(solution)/shard_map/all_gather | solution.py:26
  581.6 1.2 copy-start.1
  584.1 1.2 copy-start
Sparse Core Ops, SparseCore 0:
  9.9 27.4 reduce-scatter.1
  52.1 16.8 all-gather.9
  74.5 124.4 all-gather.11
  201.0 122.6 all-gather.17
  325.6 122.6 all-gather.15
  450.3 122.6 all-gather.13
